TPU v7x, 512 devices: a whole 4x4x16 slice. The times are simulated.
512 devices in a mesh: gx: 32 (over z, core), gy: 4 (over x), gz: 4 (over y).
Axes of the slice: x: 4, y: 4, z: 16, core: 2. Of those that a mesh axis runs over, the one named last changes fastest.
Arguments:
- adjoint_final: float32 [16, 512, 512], P('gz', 'gx', 'gy'), may hold values from -6 to 6
- conductivity: float32 [3, 16, 512, 512], P(None, 'gz', 'gx', 'gy'), may hold values from 0.05 to 1
- step_ratio: float32 [16, 512, 512], P('gz', 'gx', 'gy'), may hold values from 0.04 to 0.16
- refine_rate: float32 [16, 512, 512], P('gz', 'gx', 'gy'), may hold values from 0.05 to 0.24
- residual: float32 [4, 8192], P(None, ('gx', 'gy')), may hold values from -6 to 6
- sensor_tile: int32 [8192], P(('gx', 'gy')), may hold values from 0 to 127, as said below
- sensor_cell: int32 [8192], P(('gx', 'gy')), may hold values from 0 to 32767
- substeps: int32 [32, 4], replicated, may hold values from 1 to 6, as said below
Outputs:
- adjoint_start: float32 [16, 512, 512], P('gz', 'gx', 'gy')
- sensitivity: float32 [16, 512, 512], P('gz', 'gx', 'gy')
Inputs may be any that keep to these rules, and one draw needn't show every extreme that they name: `sensor_tile`: tiles are numbered ix * 4 + iy. Among the 64 sensors of each aligned block at most 4 name one tile, and in every block some tile is named by exactly 4 of them. `substeps`: some tile takes 6 sub-steps in every draw.
All inputs are finite; a program needn't handle non-finite values.
Results may differ from a plain program's by a relative error of at most 0.000079.
Values sent between devices are 32-bit elements; how exact they have to be, the bound alone decides.
No kernel may reach another device: no remote copies, remote signals or barrier semaphores. Data moves between devices by JAX's collectives and lax.ppermute only.
A program may use at most 64 MiB of HBM per device.

v0:
```python
import jax
import jax.numpy as jnp
from jax import lax
from jax.sharding import PartitionSpec as P


def with_halo(cells, sides, width):
    for axis, dim in sides:
        count = lax.axis_size(axis)
        ends = count - 1
        head = lax.slice_in_dim(cells, 0, width, axis=dim)
        tail = lax.slice_in_dim(cells, cells.shape[dim] - width, cells.shape[dim], axis=dim)
        cells = jnp.concatenate(
            [
                lax.ppermute(tail, axis, [(i, (i + 1) % count) for i in range(ends)]),
                cells,
                lax.ppermute(head, axis, [((i + 1) % count, i) for i in range(ends)]),
            ],
            axis=dim,
        )
    return cells


def harmonic(first, second):
    return 2.0 * first * second / (first + second)


def lateral(field):
    down_diff = field[:, 1:, :] - field[:, :-1, :]
    side_diff = field[:, :, 1:] - field[:, :, :-1]
    rows_part = jnp.pad(down_diff, ((0, 0), (0, 1), (0, 0))) - jnp.pad(
        down_diff, ((0, 0), (1, 0), (0, 0))
    )
    cols_part = jnp.pad(side_diff, ((0, 0), (0, 0), (0, 1))) - jnp.pad(
        side_diff, ((0, 0), (0, 0), (1, 0))
    )
    return rows_part + cols_part


def refine(field, rates, count):

    def one_turn(turn, state):
        return state + lateral(rates * state)

    return lax.fori_loop(jnp.int32(0), count, one_turn, field)


def body(
    adjoint_final,
    conductivity,
    step_ratio,
    refine_rate,
    residual,
    sensor_tile,
    sensor_cell,
    substeps,
):
    layers, rows, cols = adjoint_final.shape
    steps = residual.shape[0]
    cells = layers * rows * cols
    row_dev = lax.axis_index("gx")
    col_dev = lax.axis_index("gy")
    layer_dev = lax.axis_index("gz")
    my_tile = row_dev * lax.axis_size("gy") + col_dev
    offset = layer_dev * cells
    padded = with_halo(conductivity, (("gx", 2), ("gy", 3), ("gz", 1)), 1)
    row_up = harmonic(conductivity[0], padded[0, 1:-1, 2:, 1:-1])
    row_down = harmonic(conductivity[0], padded[0, 1:-1, :-2, 1:-1])
    col_up = harmonic(conductivity[1], padded[1, 1:-1, 1:-1, 2:])
    col_down = harmonic(conductivity[1], padded[1, 1:-1, 1:-1, :-2])
    layer_up = harmonic(conductivity[2], padded[2, 2:, 1:-1, 1:-1])
    layer_down = harmonic(conductivity[2], padded[2, :-2, 1:-1, 1:-1])
    got_res, got_tile, got_cell = (
        lax.all_gather(residual, ("gx", "gy"), axis=1, tiled=True),
        lax.all_gather(sensor_tile.astype(jnp.float32), ("gx", "gy"), axis=0, tiled=True),
        lax.all_gather(sensor_cell.astype(jnp.float32), ("gx", "gy"), axis=0, tiled=True),
    )
    local_cell = got_cell.astype(jnp.int32) - offset
    keep = (got_tile.astype(jnp.int32) == my_tile) & (local_cell >= 0) & (local_cell < cells)
    index_of = jnp.where(keep, local_cell, 0)
    values_all = jnp.where(keep[None, :], got_res, 0.0)
    source = jnp.zeros((steps, cells), jnp.float32).at[:, index_of].add(values_all)
    my_count = substeps[row_dev, col_dev]
    adjoint = adjoint_final
    sensitivity = jnp.zeros_like(adjoint_final)
    for step_index in range(steps - 1, -1, -1):
        adjoint = adjoint + source[step_index].reshape(layers, rows, cols)
        weighted = step_ratio * adjoint
        wpad = with_halo(weighted, (("gx", 1), ("gy", 2), ("gz", 0)), 1)
        adjoint = adjoint + (
            row_up * (wpad[1:-1, 2:, 1:-1] - weighted)
            + row_down * (wpad[1:-1, :-2, 1:-1] - weighted)
            + col_up * (wpad[1:-1, 1:-1, 2:] - weighted)
            + col_down * (wpad[1:-1, 1:-1, :-2] - weighted)
            + layer_up * (wpad[2:, 1:-1, 1:-1] - weighted)
            + layer_down * (wpad[:-2, 1:-1, 1:-1] - weighted)
        )
        adjoint = refine(adjoint, refine_rate, my_count)
        sensitivity = sensitivity + step_ratio * adjoint
    return (adjoint, sensitivity)


def solution(mesh):
    return jax.shard_map(
        body,
        mesh=mesh,
        in_specs=(
            P("gz", "gx", "gy"),
            P(None, "gz", "gx", "gy"),
            P("gz", "gx", "gy"),
            P("gz", "gx", "gy"),
            P(None, ("gx", "gy")),
            P(("gx", "gy")),
            P(("gx", "gy")),
            P(),
        ),
        out_specs=(P("gz", "gx", "gy"), P("gz", "gx", "gy")),
        check_vma=False,
    )
```

profile of v0, /device:TPU:154, one launch (start us, length us, event | category | flops | bytes accessed | tf_op | source)
XLA Modules:
  0.0 543.7 jit_solution(5901369545518691948)
XLA Ops:
  16.5 174.7 %all-gather = f32[128,64,4]{1,2,0:T(4,128)S(1)} all-gather(f32[1,64,4]{1,2,0:T(4,128)} %bitcast.87), channel_id=1, replica_groups=mesh['gx'=32,'gy'=4,'gz'=4] {'gx','gy'}, dimensions={0}, use_global_device_ids=true | all-gather | bytes 132096 | tf_op jit(solution)/shard_map/all_gather | solution.py:74
  195.3 3.0 collective-permute-start.6
  198.3 133.8 %all-reduce.21.cloned.1.call-done = (f32[8192]{0:T(1024)}, f32[8192]{0:T(1024)}) async-done(((f32[8192]{0:T(1024)}, f32[8192]{0:T(1024)}), (f32[8192]{0:T(1024)}, f32[8192]{0:T(1024)})) %all-reduce.21.cloned.1.call-update) | async-done | bytes 65552
  335.6 59.4 %scatter_custom_fusion = f32[4,8192]{0,1:T(8,128)} fusion(s32[8192]{0:T(1024)S(1)} %get-tuple-element.283, f32[8192,4]{1,0:T(8,128)} %copy.13, f32[]{:T(128)} %constant.63.clone.1), kind=kCustom, calls=%fused_computation.17 | custom fusion | flops 32768 | bytes 131584 | tf_op jit(solution)/shard_map/scatter-add | solution.py:82
  395.1 14.0 %slice_reduce_fusion = (f32[8192]{0:T(1024)S(1)}, f32[8192]{0:T(1024)S(1)}, f32[8192]{0:T(1024)S(1)}, f32[8192]{0:T(1024)S(1)}) fusion(f32[4,8192]{0,1:T(8,128)} %scatter_custom_fusion), kind=kLoop, calls=%fused_computation.13 | loop fusion | bytes 262144 | tf_op jit(solution)/shard_map/slice | solution.py:87
  409.1 3.7 collective-permute-start.1
  414.9 4.0 collective-permute-done.3
  421.5 3.3 collective-permute-start.7
  426.1 4.5 collective-permute-start.8
  432.1 4.5 collective-permute-start.9
  438.4 5.6 %while.48 = (s32[]{:T(128)}, f32[4,16,128]{2,1,0:T(8,128)S(1)}, s32[]{:T(128)}, f32[4,16,128]{2,1,0:T(8,128)S(1)}, s32[]{:T(128)}) while((s32[]{:T(128)}, f32[4,16,128]{2,1,0:T(8,128)S(1)}, s32[]{:T(128)}, f32[4,16,128]{2,1,0:T(8,128)S(1)}, s32[]{:T(128)}) %tuple.137), condition=%wide.region_2.3_spmd, body=%wide.region_1.2_spmd.sunk | while | flops 56770 | bytes 416829 | solution.py:45
  448.4 3.7 collective-permute-done.13
  454.1 3.9 collective-permute-start.15
  460.1 4.2 collective-permute-start.16
  465.9 4.2 collective-permute-done.17
  470.2 5.6 %while.49 = (s32[]{:T(128)}, f32[4,16,128]{2,1,0:T(8,128)S(1)}, s32[]{:T(128)}, f32[4,16,128]{2,1,0:T(8,128)S(1)}, s32[]{:T(128)}) while((s32[]{:T(128)}, f32[4,16,128]{2,1,0:T(8,128)S(1)}, s32[]{:T(128)}, f32[4,16,128]{2,1,0:T(8,128)S(1)}, s32[]{:T(128)}) %tuple.138), condition=%wide.region_4.5_spmd, body=%wide.region_3.4_spmd.sunk | while | flops 56770 | bytes 416829 | solution.py:45
  480.2 3.7 collective-permute-done.19
  485.9 3.9 collective-permute-start.21
  496.2 4.2 collective-permute-done.23
  500.6 5.6 %while.50 = (s32[]{:T(128)}, f32[4,16,128]{2,1,0:T(8,128)S(1)}, s32[]{:T(128)}, f32[4,16,128]{2,1,0:T(8,128)S(1)}, s32[]{:T(128)}) while((s32[]{:T(128)}, f32[4,16,128]{2,1,0:T(8,128)S(1)}, s32[]{:T(128)}, f32[4,16,128]{2,1,0:T(8,128)S(1)}, s32[]{:T(128)}) %tuple.139), condition=%wide.region_6.7_spmd, body=%wide.region_5.6_spmd.sunk | while | flops 56770 | bytes 416829 | solution.py:45
  510.5 3.7 collective-permute-done.25
  516.2 3.9 collective-permute-start.27
  526.2 4.2 collective-permute-done.29
  530.6 5.6 %while.51 = (s32[]{:T(128)}, f32[4,16,128]{2,1,0:T(8,128)S(1)}, s32[]{:T(128)}, f32[4,16,128]{2,1,0:T(8,128)S(1)}, s32[]{:T(128)}) while((s32[]{:T(128)}, f32[4,16,128]{2,1,0:T(8,128)S(1)}, s32[]{:T(128)}, f32[4,16,128]{2,1,0:T(8,128)S(1)}, s32[]{:T(128)}) %tuple.140), condition=%wide.region_8.9_spmd, body=%wide.region_7.8_spmd.sunk | while | flops 56770 | bytes 416829 | solution.py:45
  (196 shorter events, 65.5 us)
Async XLA Ops:
  7.2 325.0 %all-reduce.21.cloned.1.call-start = ((), (), s32[]{:S(2)}) async-start(), calls=%async_computation | async-start | bytes 131072
  8.0 183.4 %collective-permute-start = (f32[3,4,1,128]{3,2,1,0:T(1,128)S(1)}, f32[3,4,1,128]{3,2,1,0:T(1,128)S(1)}, u32[]{:S(2)}, u32[]{:S(2)}) collective-permute-start(f32[3,4,1,128]{3,2,1,0:T(1,128)S(1)} %get-tuple-element.298), channel_id=1, source_target_pairs={{16,0},{32,16},{48,32},{64,48},{80,64},{96,80},{112,96},{128,112},... | collective-permute-start | bytes 18440 | tf_op jit(solution)/shard_map/ppermute | solution.py:17
  10.0 181.4 %collective-permute-start.2 = (f32[3,4,1,128]{3,2,1,0:T(1,128)S(1)}, f32[3,4,1,128]{3,2,1,0:T(1,128)S(1)}, u32[]{:S(2)}, u32[]{:S(2)}) collective-permute-start(f32[3,4,1,128]{3,2,1,0:T(1,128)S(1)} %get-tuple-element.297), channel_id=1, source_target_pairs={{0,16},{16,32},{32,48},{48,64},{64,80},{80,96},{96,112},{112,128},... | collective-permute-start | bytes 18440 | tf_op jit(solution)/shard_map/ppermute | solution.py:15
  192.5 222.3 %collective-permute-start.4 = (f32[3,4,18,1]{3,2,1,0:T(8,128)S(1)}, f32[3,4,18,1]{3,2,1,0:T(8,128)S(1)}, u32[]{:S(2)}, u32[]{:S(2)}) collective-permute-start(f32[3,4,18,1]{3,2,1,0:T(8,128)S(1)} %get-tuple-element.288), channel_id=1, source_target_pairs={{4,0},{8,4},{12,8},{5,1},{9,5},{13,9},{6,2},{10,6},{14,10},{7,3},{... | collective-permute-start | bytes 2600 | tf_op jit(solution)/shard_map/ppermute | solution.py:17
  195.3 219.4 %collective-permute-start.6 = (f32[3,4,18,1]{3,2,1,0:T(8,128)S(1)}, f32[3,4,18,1]{3,2,1,0:T(8,128)S(1)}, u32[]{:S(2)}, u32[]{:S(2)}) collective-permute-start(f32[3,4,18,1]{3,2,1,0:T(8,128)S(1)} %get-tuple-element.287), channel_id=1, source_target_pairs={{0,4},{4,8},{8,12},{1,5},{5,9},{9,13},{2,6},{6,10},{10,14},{3,7},{... | collective-permute-start | bytes 2600 | tf_op jit(solution)/shard_map/ppermute | solution.py:15
  409.1 5.8 %collective-permute-start.1 = (f32[4,1,128]{2,1,0:T(1,128)S(1)}, f32[4,1,128]{2,1,0:T(1,128)S(1)}, u32[]{:S(2)}, u32[]{:S(2)}) collective-permute-start(f32[4,1,128]{2,1,0:T(1,128)S(1)} %get-tuple-element.314), channel_id=1, source_target_pairs={{16,0},{32,16},{48,32},{64,48},{80,64},{96,80},{112,96},{128,112},... | collective-permute-start | bytes 6152 | tf_op jit(solution)/shard_map/ppermute | solution.py:17
  412.8 6.1 %collective-permute-start.3 = (f32[4,1,128]{2,1,0:T(1,128)S(1)}, f32[4,1,128]{2,1,0:T(1,128)S(1)}, u32[]{:S(2)}, u32[]{:S(2)}) collective-permute-start(f32[4,1,128]{2,1,0:T(1,128)S(1)} %get-tuple-element.313), channel_id=1, source_target_pairs={{0,16},{16,32},{32,48},{48,64},{64,80},{80,96},{96,112},{112,128},... | collective-permute-start | bytes 6152 | tf_op jit(solution)/shard_map/ppermute | solution.py:15
  419.0 11.7 %collective-permute-start.5 = (f32[4,18,1]{2,1,0:T(8,128)S(1)}, f32[4,18,1]{2,1,0:T(8,128)S(1)}, u32[]{:S(2)}, u32[]{:S(2)}) collective-permute-start(f32[4,18,1]{2,1,0:T(8,128)S(1)} %get-tuple-element.306), channel_id=1, source_target_pairs={{4,0},{8,4},{12,8},{5,1},{9,5},{13,9},{6,2},{10,6},{14,10},{7,3},{... | collective-permute-start | bytes 872 | tf_op jit(solution)/shard_map/ppermute | solution.py:17
  421.5 9.2 %collective-permute-start.7 = (f32[4,18,1]{2,1,0:T(8,128)S(1)}, f32[4,18,1]{2,1,0:T(8,128)S(1)}, u32[]{:S(2)}, u32[]{:S(2)}) collective-permute-start(f32[4,18,1]{2,1,0:T(8,128)S(1)} %get-tuple-element.305), channel_id=1, source_target_pairs={{0,4},{4,8},{8,12},{1,5},{5,9},{9,13},{2,6},{6,10},{10,14},{3,7},{... | collective-permute-start | bytes 872 | tf_op jit(solution)/shard_map/ppermute | solution.py:15
  424.8 13.2 %collective-permute-start.10 = (f32[3,1,18,130]{3,2,1,0:T(8,128)S(1)}, f32[3,1,18,130]{3,2,1,0:T(8,128)S(1)}, u32[]{:S(2)}, u32[]{:S(2)}) collective-permute-start(f32[3,1,18,130]{3,2,1,0:T(8,128)S(1)} %get-tuple-element.285), channel_id=1, source_target_pairs={{0,1},{1,2},{2,3},{4,5},{5,6},{6,7},{8,9},{9,10},{10,11},{12,13},{... | collective-permute-start | bytes 84248 | tf_op jit(solution)/shard_map/ppermute | solution.py:15
  426.1 11.9 %collective-permute-start.8 = (f32[3,1,18,130]{3,2,1,0:T(8,128)S(1)}, f32[3,1,18,130]{3,2,1,0:T(8,128)S(1)}, u32[]{:S(2)}, u32[]{:S(2)}) collective-permute-start(f32[3,1,18,130]{3,2,1,0:T(8,128)S(1)} %get-tuple-element.286), channel_id=1, source_target_pairs={{1,0},{2,1},{3,2},{5,4},{6,5},{7,6},{9,8},{10,9},{11,10},{13,12},{... | collective-permute-start | bytes 84248 | tf_op jit(solution)/shard_map/ppermute | solution.py:17
  430.8 7.2 %collective-permute-start.11 = (f32[1,18,130]{2,1,0:T(8,128)S(1)}, f32[1,18,130]{2,1,0:T(8,128)S(1)}, u32[]{:S(2)}, u32[]{:S(2)}) collective-permute-start(f32[1,18,130]{2,1,0:T(8,128)S(1)} %get-tuple-element.296), channel_id=1, source_target_pairs={{0,1},{1,2},{2,3},{4,5},{5,6},{6,7},{8,9},{9,10},{10,11},{12,13},{... | collective-permute-start | bytes 28088 | tf_op jit(solution)/shard_map/ppermute | solution.py:15
  432.1 6.1 %collective-permute-start.9 = (f32[1,18,130]{2,1,0:T(8,128)S(1)}, f32[1,18,130]{2,1,0:T(8,128)S(1)}, u32[]{:S(2)}, u32[]{:S(2)}) collective-permute-start(f32[1,18,130]{2,1,0:T(8,128)S(1)} %get-tuple-element.295), channel_id=1, source_target_pairs={{1,0},{2,1},{3,2},{5,4},{6,5},{7,6},{9,8},{10,9},{11,10},{13,12},{... | collective-permute-start | bytes 28088 | tf_op jit(solution)/shard_map/ppermute | solution.py:17
  445.9 6.1 %collective-permute-start.13 = (f32[4,1,128]{2,1,0:T(1,128)S(1)}, f32[4,1,128]{2,1,0:T(1,128)S(1)}, u32[]{:S(2)}, u32[]{:S(2)}) collective-permute-start(f32[4,1,128]{2,1,0:T(1,128)S(1)} %get-tuple-element.311), channel_id=1, source_target_pairs={{0,16},{16,32},{32,48},{48,64},{64,80},{80,96},{96,112},{112,128},... | collective-permute-start | bytes 6152 | tf_op jit(solution)/shard_map/ppermute | solution.py:15
  452.1 6.0 %collective-permute-start.14 = (f32[4,18,1]{2,1,0:T(8,128)S(1)}, f32[4,18,1]{2,1,0:T(8,128)S(1)}, u32[]{:S(2)}, u32[]{:S(2)}) collective-permute-start(f32[4,18,1]{2,1,0:T(8,128)S(1)} %get-tuple-element.304), channel_id=1, source_target_pairs={{4,0},{8,4},{12,8},{5,1},{9,5},{13,9},{6,2},{10,6},{14,10},{7,3},{... | collective-permute-start | bytes 872 | tf_op jit(solution)/shard_map/ppermute | solution.py:17
  454.1 6.0 %collective-permute-start.15 = (f32[4,18,1]{2,1,0:T(8,128)S(1)}, f32[4,18,1]{2,1,0:T(8,128)S(1)}, u32[]{:S(2)}, u32[]{:S(2)}) collective-permute-start(f32[4,18,1]{2,1,0:T(8,128)S(1)} %get-tuple-element.303), channel_id=1, source_target_pairs={{0,4},{4,8},{8,12},{1,5},{5,9},{9,13},{2,6},{6,10},{10,14},{3,7},{... | collective-permute-start | bytes 872 | tf_op jit(solution)/shard_map/ppermute | solution.py:15
  460.1 5.7 %collective-permute-start.16 = (f32[1,18,130]{2,1,0:T(8,128)S(1)}, f32[1,18,130]{2,1,0:T(8,128)S(1)}, u32[]{:S(2)}, u32[]{:S(2)}) collective-permute-start(f32[1,18,130]{2,1,0:T(8,128)S(1)} %get-tuple-element.293), channel_id=1, source_target_pairs={{1,0},{2,1},{3,2},{5,4},{6,5},{7,6},{9,8},{10,9},{11,10},{13,12},{... | collective-permute-start | bytes 28088 | tf_op jit(solution)/shard_map/ppermute | solution.py:17
  464.4 5.7 %collective-permute-start.17 = (f32[1,18,130]{2,1,0:T(8,128)S(1)}, f32[1,18,130]{2,1,0:T(8,128)S(1)}, u32[]{:S(2)}, u32[]{:S(2)}) collective-permute-start(f32[1,18,130]{2,1,0:T(8,128)S(1)} %get-tuple-element.294), channel_id=1, source_target_pairs={{0,1},{1,2},{2,3},{4,5},{5,6},{6,7},{8,9},{9,10},{10,11},{12,13},{... | collective-permute-start | bytes 28088 | tf_op jit(solution)/shard_map/ppermute | solution.py:15
  477.8 6.1 %collective-permute-start.19 = (f32[4,1,128]{2,1,0:T(1,128)S(1)}, f32[4,1,128]{2,1,0:T(1,128)S(1)}, u32[]{:S(2)}, u32[]{:S(2)}) collective-permute-start(f32[4,1,128]{2,1,0:T(1,128)S(1)} %get-tuple-element.309), channel_id=1, source_target_pairs={{0,16},{16,32},{32,48},{48,64},{64,80},{80,96},{96,112},{112,128},... | collective-permute-start | bytes 6152 | tf_op jit(solution)/shard_map/ppermute | solution.py:15
  484.0 6.0 %collective-permute-start.20 = (f32[4,18,1]{2,1,0:T(8,128)S(1)}, f32[4,18,1]{2,1,0:T(8,128)S(1)}, u32[]{:S(2)}, u32[]{:S(2)}) collective-permute-start(f32[4,18,1]{2,1,0:T(8,128)S(1)} %get-tuple-element.302), channel_id=1, source_target_pairs={{4,0},{8,4},{12,8},{5,1},{9,5},{13,9},{6,2},{10,6},{14,10},{7,3},{... | collective-permute-start | bytes 872 | tf_op jit(solution)/shard_map/ppermute | solution.py:17
  485.9 6.0 %collective-permute-start.21 = (f32[4,18,1]{2,1,0:T(8,128)S(1)}, f32[4,18,1]{2,1,0:T(8,128)S(1)}, u32[]{:S(2)}, u32[]{:S(2)}) collective-permute-start(f32[4,18,1]{2,1,0:T(8,128)S(1)} %get-tuple-element.301), channel_id=1, source_target_pairs={{0,4},{4,8},{8,12},{1,5},{5,9},{9,13},{2,6},{6,10},{10,14},{3,7},{... | collective-permute-start | bytes 872 | tf_op jit(solution)/shard_map/ppermute | solution.py:15
  508.1 6.1 %collective-permute-start.25 = (f32[4,1,128]{2,1,0:T(1,128)S(1)}, f32[4,1,128]{2,1,0:T(1,128)S(1)}, u32[]{:S(2)}, u32[]{:S(2)}) collective-permute-start(f32[4,1,128]{2,1,0:T(1,128)S(1)} %get-tuple-element.307), channel_id=1, source_target_pairs={{0,16},{16,32},{32,48},{48,64},{64,80},{80,96},{96,112},{112,128},... | collective-permute-start | bytes 6152 | tf_op jit(solution)/shard_map/ppermute | solution.py:15
  514.3 6.0 %collective-permute-start.26 = (f32[4,18,1]{2,1,0:T(8,128)S(1)}, f32[4,18,1]{2,1,0:T(8,128)S(1)}, u32[]{:S(2)}, u32[]{:S(2)}) collective-permute-start(f32[4,18,1]{2,1,0:T(8,128)S(1)} %get-tuple-element.300), channel_id=1, source_target_pairs={{4,0},{8,4},{12,8},{5,1},{9,5},{13,9},{6,2},{10,6},{14,10},{7,3},{... | collective-permute-start | bytes 872 | tf_op jit(solution)/shard_map/ppermute | solution.py:17
  516.2 6.0 %collective-permute-start.27 = (f32[4,18,1]{2,1,0:T(8,128)S(1)}, f32[4,18,1]{2,1,0:T(8,128)S(1)}, u32[]{:S(2)}, u32[]{:S(2)}) collective-permute-start(f32[4,18,1]{2,1,0:T(8,128)S(1)} %get-tuple-element.299), channel_id=1, source_target_pairs={{0,4},{4,8},{8,12},{1,5},{5,9},{9,13},{2,6},{6,10},{10,14},{3,7},{... | collective-permute-start | bytes 872 | tf_op jit(solution)/shard_map/ppermute | solution.py:15
  (14 other events, 125.7 us)
Sparse Core Ops, SparseCore 0:
  16.7 315.4 all-reduce.20
where the time goes:
time: 545 us; the launch traced here: 544 us
  blocking collectives  175 us (32%)
  waiting for transfers between devices  168 us (31%)
  starting transfers between devices  77 us (14%)
  other arithmetic  68.6 us (13%)
  local copies, waits for them, and re-layouts  21.3 us (4%)
  loops' own time  18.2 us (3%)
  between operations  15.3 us (3%)
    all_gather x1, blocking collectives, body(): lax.all_gather(residual, ('gx', 'gy'), axis=1, tiled=True)  175 us
    unnamed x2, waiting for transfers between devices  134 us
    scatter-add x1, other arithmetic, body(): jnp.zeros((steps, cells), jnp.float32).at[:, index_of].add(values_all)  59.4 us
    ppermute x15, starting transfers between devices, with_halo(): lax.ppermute(head, axis, [((i + 1) % count, i) for i in range(ends)])  40.9 us
    ppermute x15, starting transfers between devices, with_halo(): lax.ppermute(tail, axis, [(i, (i + 1) % count) for i in range(ends)])  36.1 us
    ppermute x15, waiting for transfers between devices, with_halo(): lax.ppermute(tail, axis, [(i, (i + 1) % count) for i in range(ends)])  33.5 us
    another operation x4, loops' own time, refine(): return lax.fori_loop(jnp.int32(0), count, one_turn, field)  18.2 us
    slice x1, local copies, waits for them, and re-layouts, body(): adjoint = adjoint + source[step_index].reshape(layers, rows, cols)  14 us
  transfers between devices with their start and end apart: 31, of which 18 were waited for; matrix products, arithmetic and copies ran while one was open for 15% of the time, Pallas kernels for 0%

commit v1 on v0

--- a/solution.py
+++ b/solution.py
@@ -71,7 +71,10 @@
     layer_up = harmonic(conductivity[2], padded[2, 2:, 1:-1, 1:-1])
     layer_down = harmonic(conductivity[2], padded[2, :-2, 1:-1, 1:-1])
     got_res, got_tile, got_cell = (
-        lax.all_gather(residual, ("gx", "gy"), axis=1, tiled=True),
+        jnp.concatenate(
+            lax.all_to_all(jnp.stack([residual] * lax.axis_size(("gx", "gy"))), ("gx", "gy"), 0, 0),
+            axis=1,
+        ),
         lax.all_gather(sensor_tile.astype(jnp.float32), ("gx", "gy"), axis=0, tiled=True),
         lax.all_gather(sensor_cell.astype(jnp.float32), ("gx", "gy"), axis=0, tiled=True),
     )

time: 545 us -> 573 us (1.051)
  blocking collectives: 175 us -> 0 us
  waiting for transfers between devices: 168 us -> 342 us
  starting transfers between devices: 77 us -> 94.7 us
  other arithmetic: 68.6 us -> 77.3 us
    all_gather x1 -> x0, blocking collectives: 175 us -> none  [body(): lax.all_gather(residual, ('gx', 'gy'), axis=1, tiled=True)]
    unnamed x2, waiting for transfers between devices: 134 us -> 307 us
    all_to_all x0 -> x1, starting transfers between devices: none -> 17.7 us  [body(): lax.all_to_all(jnp.stack([residual] * lax.axis_size(('gx', 'gy'))), ('gx'...]
    select_n x1, other arithmetic: 0.05 us -> 7.45 us  [body(): values_all = jnp.where(keep[None, :], got_res, 0.0)]
  transfers between devices with their start and end apart: 31 -> 32, of which waited for: 18 -> 18; matrix products, arithmetic and copies ran while one was open for 15% -> 16% of each run, Pallas kernels for 0% -> 0%
where the time goes in v1:
time: 573 us; the launch traced here: 572 us
  waiting for transfers between devices  342 us (60%)
  starting transfers between devices  94.7 us (17%)
  other arithmetic  77.3 us (13%)
  local copies, waits for them, and re-layouts  23.6 us (4%)
  loops' own time  18.6 us (3%)
  between operations  15.3 us (3%)
    unnamed x2, waiting for transfers between devices  307 us
    scatter-add x1, other arithmetic, body(): jnp.zeros((steps, cells), jnp.float32).at[:, index_of].add(values_all)  59.7 us
    ppermute x15, starting transfers between devices, with_halo(): lax.ppermute(head, axis, [((i + 1) % count, i) for i in range(ends)])  40.8 us
    ppermute x15, starting transfers between devices, with_halo(): lax.ppermute(tail, axis, [(i, (i + 1) % count) for i in range(ends)])  36.2 us
    ppermute x15, waiting for transfers between devices, with_halo(): lax.ppermute(tail, axis, [(i, (i + 1) % count) for i in range(ends)])  33.5 us
    another operation x4, loops' own time, refine(): return lax.fori_loop(jnp.int32(0), count, one_turn, field)  18.6 us
    all_to_all x1, starting transfers between devices, body(): lax.all_to_all(jnp.stack([residual] * lax.axis_size(('gx', 'gy'))), ('gx'...  17.7 us
    slice x1, local copies, waits for them, and re-layouts, body(): adjoint = adjoint + source[step_index].reshape(layers, rows, cols)  14 us
  transfers between devices with their start and end apart: 32, of which 18 were waited for; matrix products, arithmetic and copies ran while one was open for 16% of the time, Pallas kernels for 0%

profile of v1, /device:TPU:154, one launch (start us, length us, event | category | flops | bytes accessed | tf_op | source)
XLA Modules:
  0.0 571.7 jit_solution(8727678282753523239)
XLA Ops:
  8.8 17.7 %all-to-all-start = ((f32[128,1,256]{2,1,0:T(1,128)}), f32[128,1,256]{2,1,0:T(1,128)S(1)}, u32[]{:S(2)}, u32[]{:S(2)}) async-start(f32[128,1,256]{2,1,0:T(1,128)} %reshape.40), calls=%async_computation | async-start | bytes 262144 | tf_op jit(solution)/shard_map/all_to_all | solution.py:75
  39.4 3.4 collective-permute-start.6
  42.8 307.5 %all-reduce.21.cloned.1.call-done = (f32[8192]{0:T(1024)}, f32[8192]{0:T(1024)}) async-done(((f32[8192]{0:T(1024)}, f32[8192]{0:T(1024)}), (f32[8192]{0:T(1024)}, f32[8192]{0:T(1024)})) %all-reduce.21.cloned.1.call-update) | async-done | bytes 65552
  355.5 7.4 %bitcast_select_fusion = f32[4,8192]{0,1:T(8,128)} fusion(f32[4,128,64]{0,2,1:T(8,128)} %copy.12, pred[8192]{0:T(1024)(128)(4,1)S(1)} %get-tuple-element.284), kind=kLoop, calls=%fused_computation.19 | loop fusion | flops 32768 | bytes 270336 | tf_op jit(solution)/shard_map/jit(_where)/select_n | solution.py:84
  363.0 59.7 %scatter_custom_fusion = f32[4,8192]{0,1:T(8,128)} fusion(s32[8192]{0:T(1024)S(1)} %get-tuple-element.283, f32[4,8192]{0,1:T(8,128)} %bitcast_select_fusion, f32[]{:T(128)} %constant.63.clone.1), kind=kCustom, calls=%fused_computation.17 | custom fusion | flops 32768 | bytes 262148 | tf_op jit(solution)/shard_map/scatter-add | solution.py:85
  422.7 14.0 %slice_reduce_fusion = (f32[8192]{0:T(1024)S(1)}, f32[8192]{0:T(1024)S(1)}, f32[8192]{0:T(1024)S(1)}, f32[8192]{0:T(1024)S(1)}) fusion(f32[4,8192]{0,1:T(8,128)} %scatter_custom_fusion), kind=kLoop, calls=%fused_computation.13 | loop fusion | bytes 262144 | tf_op jit(solution)/shard_map/slice | solution.py:90
  436.7 3.7 collective-permute-start.1
  442.5 4.0 collective-permute-done.3
  453.8 4.5 collective-permute-start.8
  459.7 4.5 collective-permute-start.9
  466.0 5.7 while.48
  476.1 3.7 collective-permute-done.13
  481.8 3.9 collective-permute-start.15
  487.9 4.2 collective-permute-start.16
  493.6 4.2 collective-permute-done.17
  497.9 5.7 while.49
  508.0 3.7 collective-permute-done.19
  513.7 3.9 collective-permute-start.21
  524.0 4.2 collective-permute-done.23
  528.4 5.7 while.50
  538.4 3.7 collective-permute-done.25
  544.1 3.9 collective-permute-start.27
  554.1 4.2 collective-permute-done.29
  558.5 5.7 while.51
  (200 shorter events, 71.6 us)
Async XLA Ops:
  8.8 342.3 %all-to-all-start = ((f32[128,1,256]{2,1,0:T(1,128)}), f32[128,1,256]{2,1,0:T(1,128)S(1)}, u32[]{:S(2)}, u32[]{:S(2)}) async-start(f32[128,1,256]{2,1,0:T(1,128)} %reshape.40), calls=%async_computation | async-start | bytes 262144 | tf_op jit(solution)/shard_map/all_to_all | solution.py:75
  26.5 323.8 %all-reduce.21.cloned.1.call-start = ((), (), s32[]{:S(2)}) async-start(), calls=%async_computation.1 | async-start | bytes 131072
  27.4 8.5 %collective-permute-start = (f32[3,4,1,128]{3,2,1,0:T(1,128)S(1)}, f32[3,4,1,128]{3,2,1,0:T(1,128)S(1)}, u32[]{:S(2)}, u32[]{:S(2)}) collective-permute-start(f32[3,4,1,128]{3,2,1,0:T(1,128)S(1)} %get-tuple-element.298), channel_id=1, source_target_pairs={{16,0},{32,16},{48,32},{64,48},{80,64},{96,80},{112,96},{128,112},... | collective-permute-start | bytes 18440 | tf_op jit(solution)/shard_map/ppermute | solution.py:17
  29.6 6.3 %collective-permute-start.2 = (f32[3,4,1,128]{3,2,1,0:T(1,128)S(1)}, f32[3,4,1,128]{3,2,1,0:T(1,128)S(1)}, u32[]{:S(2)}, u32[]{:S(2)}) collective-permute-start(f32[3,4,1,128]{3,2,1,0:T(1,128)S(1)} %get-tuple-element.297), channel_id=1, source_target_pairs={{0,16},{16,32},{32,48},{48,64},{64,80},{80,96},{96,112},{112,128},... | collective-permute-start | bytes 18440 | tf_op jit(solution)/shard_map/ppermute | solution.py:15
  36.9 405.4 %collective-permute-start.4 = (f32[3,4,18,1]{3,2,1,0:T(8,128)S(1)}, f32[3,4,18,1]{3,2,1,0:T(8,128)S(1)}, u32[]{:S(2)}, u32[]{:S(2)}) collective-permute-start(f32[3,4,18,1]{3,2,1,0:T(8,128)S(1)} %get-tuple-element.288), channel_id=1, source_target_pairs={{4,0},{8,4},{12,8},{5,1},{9,5},{13,9},{6,2},{10,6},{14,10},{7,3},{... | collective-permute-start | bytes 2600 | tf_op jit(solution)/shard_map/ppermute | solution.py:17
  39.4 402.9 %collective-permute-start.6 = (f32[3,4,18,1]{3,2,1,0:T(8,128)S(1)}, f32[3,4,18,1]{3,2,1,0:T(8,128)S(1)}, u32[]{:S(2)}, u32[]{:S(2)}) collective-permute-start(f32[3,4,18,1]{3,2,1,0:T(8,128)S(1)} %get-tuple-element.287), channel_id=1, source_target_pairs={{0,4},{4,8},{8,12},{1,5},{5,9},{9,13},{2,6},{6,10},{10,14},{3,7},{... | collective-permute-start | bytes 2600 | tf_op jit(solution)/shard_map/ppermute | solution.py:15
  436.7 5.8 %collective-permute-start.1 = (f32[4,1,128]{2,1,0:T(1,128)S(1)}, f32[4,1,128]{2,1,0:T(1,128)S(1)}, u32[]{:S(2)}, u32[]{:S(2)}) collective-permute-start(f32[4,1,128]{2,1,0:T(1,128)S(1)} %get-tuple-element.314), channel_id=1, source_target_pairs={{16,0},{32,16},{48,32},{64,48},{80,64},{96,80},{112,96},{128,112},... | collective-permute-start | bytes 6152 | tf_op jit(solution)/shard_map/ppermute | solution.py:17
  440.4 6.1 %collective-permute-start.3 = (f32[4,1,128]{2,1,0:T(1,128)S(1)}, f32[4,1,128]{2,1,0:T(1,128)S(1)}, u32[]{:S(2)}, u32[]{:S(2)}) collective-permute-start(f32[4,1,128]{2,1,0:T(1,128)S(1)} %get-tuple-element.313), channel_id=1, source_target_pairs={{0,16},{16,32},{32,48},{48,64},{64,80},{80,96},{96,112},{112,128},... | collective-permute-start | bytes 6152 | tf_op jit(solution)/shard_map/ppermute | solution.py:15
  446.6 11.7 %collective-permute-start.5 = (f32[4,18,1]{2,1,0:T(8,128)S(1)}, f32[4,18,1]{2,1,0:T(8,128)S(1)}, u32[]{:S(2)}, u32[]{:S(2)}) collective-permute-start(f32[4,18,1]{2,1,0:T(8,128)S(1)} %get-tuple-element.306), channel_id=1, source_target_pairs={{4,0},{8,4},{12,8},{5,1},{9,5},{13,9},{6,2},{10,6},{14,10},{7,3},{... | collective-permute-start | bytes 872 | tf_op jit(solution)/shard_map/ppermute | solution.py:17
  449.2 9.2 %collective-permute-start.7 = (f32[4,18,1]{2,1,0:T(8,128)S(1)}, f32[4,18,1]{2,1,0:T(8,128)S(1)}, u32[]{:S(2)}, u32[]{:S(2)}) collective-permute-start(f32[4,18,1]{2,1,0:T(8,128)S(1)} %get-tuple-element.305), channel_id=1, source_target_pairs={{0,4},{4,8},{8,12},{1,5},{5,9},{9,13},{2,6},{6,10},{10,14},{3,7},{... | collective-permute-start | bytes 872 | tf_op jit(solution)/shard_map/ppermute | solution.py:15
  452.5 13.1 %collective-permute-start.10 = (f32[3,1,18,130]{3,2,1,0:T(8,128)S(1)}, f32[3,1,18,130]{3,2,1,0:T(8,128)S(1)}, u32[]{:S(2)}, u32[]{:S(2)}) collective-permute-start(f32[3,1,18,130]{3,2,1,0:T(8,128)S(1)} %get-tuple-element.285), channel_id=1, source_target_pairs={{0,1},{1,2},{2,3},{4,5},{5,6},{6,7},{8,9},{9,10},{10,11},{12,13},{... | collective-permute-start | bytes 84248 | tf_op jit(solution)/shard_map/ppermute | solution.py:15
  453.8 11.8 %collective-permute-start.8 = (f32[3,1,18,130]{3,2,1,0:T(8,128)S(1)}, f32[3,1,18,130]{3,2,1,0:T(8,128)S(1)}, u32[]{:S(2)}, u32[]{:S(2)}) collective-permute-start(f32[3,1,18,130]{3,2,1,0:T(8,128)S(1)} %get-tuple-element.286), channel_id=1, source_target_pairs={{1,0},{2,1},{3,2},{5,4},{6,5},{7,6},{9,8},{10,9},{11,10},{13,12},{... | collective-permute-start | bytes 84248 | tf_op jit(solution)/shard_map/ppermute | solution.py:17
  458.4 7.2 %collective-permute-start.11 = (f32[1,18,130]{2,1,0:T(8,128)S(1)}, f32[1,18,130]{2,1,0:T(8,128)S(1)}, u32[]{:S(2)}, u32[]{:S(2)}) collective-permute-start(f32[1,18,130]{2,1,0:T(8,128)S(1)} %get-tuple-element.296), channel_id=1, source_target_pairs={{0,1},{1,2},{2,3},{4,5},{5,6},{6,7},{8,9},{9,10},{10,11},{12,13},{... | collective-permute-start | bytes 28088 | tf_op jit(solution)/shard_map/ppermute | solution.py:15
  459.7 6.1 %collective-permute-start.9 = (f32[1,18,130]{2,1,0:T(8,128)S(1)}, f32[1,18,130]{2,1,0:T(8,128)S(1)}, u32[]{:S(2)}, u32[]{:S(2)}) collective-permute-start(f32[1,18,130]{2,1,0:T(8,128)S(1)} %get-tuple-element.295), channel_id=1, source_target_pairs={{1,0},{2,1},{3,2},{5,4},{6,5},{7,6},{9,8},{10,9},{11,10},{13,12},{... | collective-permute-start | bytes 28088 | tf_op jit(solution)/shard_map/ppermute | solution.py:17
  473.6 6.1 %collective-permute-start.13 = (f32[4,1,128]{2,1,0:T(1,128)S(1)}, f32[4,1,128]{2,1,0:T(1,128)S(1)}, u32[]{:S(2)}, u32[]{:S(2)}) collective-permute-start(f32[4,1,128]{2,1,0:T(1,128)S(1)} %get-tuple-element.311), channel_id=1, source_target_pairs={{0,16},{16,32},{32,48},{48,64},{64,80},{80,96},{96,112},{112,128},... | collective-permute-start | bytes 6152 | tf_op jit(solution)/shard_map/ppermute | solution.py:15
  479.8 6.0 %collective-permute-start.14 = (f32[4,18,1]{2,1,0:T(8,128)S(1)}, f32[4,18,1]{2,1,0:T(8,128)S(1)}, u32[]{:S(2)}, u32[]{:S(2)}) collective-permute-start(f32[4,18,1]{2,1,0:T(8,128)S(1)} %get-tuple-element.304), channel_id=1, source_target_pairs={{4,0},{8,4},{12,8},{5,1},{9,5},{13,9},{6,2},{10,6},{14,10},{7,3},{... | collective-permute-start | bytes 872 | tf_op jit(solution)/shard_map/ppermute | solution.py:17
  481.8 6.0 %collective-permute-start.15 = (f32[4,18,1]{2,1,0:T(8,128)S(1)}, f32[4,18,1]{2,1,0:T(8,128)S(1)}, u32[]{:S(2)}, u32[]{:S(2)}) collective-permute-start(f32[4,18,1]{2,1,0:T(8,128)S(1)} %get-tuple-element.303), channel_id=1, source_target_pairs={{0,4},{4,8},{8,12},{1,5},{5,9},{9,13},{2,6},{6,10},{10,14},{3,7},{... | collective-permute-start | bytes 872 | tf_op jit(solution)/shard_map/ppermute | solution.py:15
  487.9 5.7 %collective-permute-start.16 = (f32[1,18,130]{2,1,0:T(8,128)S(1)}, f32[1,18,130]{2,1,0:T(8,128)S(1)}, u32[]{:S(2)}, u32[]{:S(2)}) collective-permute-start(f32[1,18,130]{2,1,0:T(8,128)S(1)} %get-tuple-element.293), channel_id=1, source_target_pairs={{1,0},{2,1},{3,2},{5,4},{6,5},{7,6},{9,8},{10,9},{11,10},{13,12},{... | collective-permute-start | bytes 28088 | tf_op jit(solution)/shard_map/ppermute | solution.py:17
  505.6 6.1 %collective-permute-start.19 = (f32[4,1,128]{2,1,0:T(1,128)S(1)}, f32[4,1,128]{2,1,0:T(1,128)S(1)}, u32[]{:S(2)}, u32[]{:S(2)}) collective-permute-start(f32[4,1,128]{2,1,0:T(1,128)S(1)} %get-tuple-element.309), channel_id=1, source_target_pairs={{0,16},{16,32},{32,48},{48,64},{64,80},{80,96},{96,112},{112,128},... | collective-permute-start | bytes 6152 | tf_op jit(solution)/shard_map/ppermute | solution.py:15
  511.8 6.0 %collective-permute-start.20 = (f32[4,18,1]{2,1,0:T(8,128)S(1)}, f32[4,18,1]{2,1,0:T(8,128)S(1)}, u32[]{:S(2)}, u32[]{:S(2)}) collective-permute-start(f32[4,18,1]{2,1,0:T(8,128)S(1)} %get-tuple-element.302), channel_id=1, source_target_pairs={{4,0},{8,4},{12,8},{5,1},{9,5},{13,9},{6,2},{10,6},{14,10},{7,3},{... | collective-permute-start | bytes 872 | tf_op jit(solution)/shard_map/ppermute | solution.py:17
  513.7 6.0 %collective-permute-start.21 = (f32[4,18,1]{2,1,0:T(8,128)S(1)}, f32[4,18,1]{2,1,0:T(8,128)S(1)}, u32[]{:S(2)}, u32[]{:S(2)}) collective-permute-start(f32[4,18,1]{2,1,0:T(8,128)S(1)} %get-tuple-element.301), channel_id=1, source_target_pairs={{0,4},{4,8},{8,12},{1,5},{5,9},{9,13},{2,6},{6,10},{10,14},{3,7},{... | collective-permute-start | bytes 872 | tf_op jit(solution)/shard_map/ppermute | solution.py:15
  536.0 6.1 %collective-permute-start.25 = (f32[4,1,128]{2,1,0:T(1,128)S(1)}, f32[4,1,128]{2,1,0:T(1,128)S(1)}, u32[]{:S(2)}, u32[]{:S(2)}) collective-permute-start(f32[4,1,128]{2,1,0:T(1,128)S(1)} %get-tuple-element.307), channel_id=1, source_target_pairs={{0,16},{16,32},{32,48},{48,64},{64,80},{80,96},{96,112},{112,128},... | collective-permute-start | bytes 6152 | tf_op jit(solution)/shard_map/ppermute | solution.py:15
  542.2 6.0 %collective-permute-start.26 = (f32[4,18,1]{2,1,0:T(8,128)S(1)}, f32[4,18,1]{2,1,0:T(8,128)S(1)}, u32[]{:S(2)}, u32[]{:S(2)}) collective-permute-start(f32[4,18,1]{2,1,0:T(8,128)S(1)} %get-tuple-element.300), channel_id=1, source_target_pairs={{4,0},{8,4},{12,8},{5,1},{9,5},{13,9},{6,2},{10,6},{14,10},{7,3},{... | collective-permute-start | bytes 872 | tf_op jit(solution)/shard_map/ppermute | solution.py:17
  544.1 6.0 %collective-permute-start.27 = (f32[4,18,1]{2,1,0:T(8,128)S(1)}, f32[4,18,1]{2,1,0:T(8,128)S(1)}, u32[]{:S(2)}, u32[]{:S(2)}) collective-permute-start(f32[4,18,1]{2,1,0:T(8,128)S(1)} %get-tuple-element.299), channel_id=1, source_target_pairs={{0,4},{4,8},{8,12},{1,5},{5,9},{9,13},{2,6},{6,10},{10,14},{3,7},{... | collective-permute-start | bytes 872 | tf_op jit(solution)/shard_map/ppermute | solution.py:15
  (15 other events, 131.5 us)
Sparse Core Ops, SparseCore 0:
  36.0 314.2 all-reduce.20
